TPU v7x, 1024 devices: a whole 8x8x8 slice. The times are simulated.
1024 devices in a mesh: lat: 32 (over z_lo, x), lon: 32 (over z_hi, y, core).
Axes of the slice: x: 8, y: 8, z: 8 (z_hi: 2, z_lo: 4; z = z_hi * 4 + z_lo), core: 2. Of those that a mesh axis runs over, the one named last changes fastest.
Arguments:
- model_state: float32 [256, 512, 960], P('lat', 'lon'), may hold values from -5 to 5
- send_slots: int32 [32, 32, 32, 4], P('lat', 'lon'), may hold values from -1 to 127, as said below
- in_weight: bfloat16 [3, 16, 406], replicated, may hold values from -0.875 to 0.875
- in_bias: float32 [406], replicated, may hold values from -4 to 4
- mid_weight: bfloat16 [406, 406], replicated, may hold values from -0.3125 to 0.3125
- mid_bias: float32 [406], replicated, may hold values from -4 to 4
- out_weight: bfloat16 [3, 406, 16], replicated, may hold values from -0.15625 to 0.15625
Outputs:
- new_state: float32 [256, 512, 960], P('lat', 'lon')
Inputs may be any that keep to these rules, and one draw needn't show every extreme that they name: send_slots[a, b, d, s] is -1 for an empty slot or a local column r * 16 + c (local row r, column c) of device (a, b) that is owned for physics by the device at longitude index d of the same latitude row; no column appears twice on a device; along each latitude row of devices every owner d receives exactly 64 live entries; on some device every slot is live.
All inputs are finite; a program needn't handle non-finite values.
Results may differ from a plain program's by a relative error of at most 0.0017.
Values may be sent and summed in bfloat16 or wider, within the bound.
A program may use at most 64 MiB of HBM per device.

v0:
```python
import math

import jax
import jax.numpy as jnp
from jax import lax
from jax.sharding import PartitionSpec as P

LEV = 60
NVAR = 16
HID = 406
FEAT = 960


courant = 0.1
phys_weight = 0.5


def with_halo(x, sides, width, wrap):
    for axis, dim in sides:
        size, length = (lax.axis_size(axis), x.shape[dim])
        up = [(i, (i + 1) % size) for i in range(size if wrap else size - 1)]
        down = [(j, i) for i, j in up]
        last = lax.slice_in_dim(x, length - width, length, axis=dim)
        first = lax.slice_in_dim(x, 0, width, axis=dim)
        before = lax.ppermute(last, axis, up)
        after = lax.ppermute(first, axis, down)
        x = jnp.concatenate([before, x, after], axis=dim)
    return x


def face_flux(lower, upper, component):
    wind_low = lower[..., component::NVAR]
    wind_high = upper[..., component::NVAR]
    speed = jnp.repeat(0.5 * (wind_low + wind_high), NVAR, axis=-1)
    return jnp.maximum(speed, 0.0) * lower + jnp.minimum(speed, 0.0) * upper


def column_physics(packets, in_weight, in_bias, mid_weight, mid_bias, out_weight):
    count = packets.shape[0]
    block_size = math.gcd(count, 64)
    stacked_out = jnp.transpose(out_weight, (1, 0, 2)).reshape(HID, 3 * NVAR)

    def one_block(block_rows):
        edge = jnp.zeros((block_size, NVAR), block_rows.dtype)
        padded = jnp.concatenate([edge, block_rows, edge], axis=1)
        summed = jnp.zeros((block_size * LEV, HID), jnp.float32)
        for tap in range(3):
            window = padded[:, tap * NVAR : tap * NVAR + FEAT].reshape(block_size * LEV, NVAR)
            summed = summed + jnp.dot(window, in_weight[tap], preferred_element_type=jnp.float32)
        first_hidden = jax.nn.silu(summed + in_bias).astype(jnp.bfloat16)
        second_hidden = jax.nn.silu(
            jnp.dot(first_hidden, mid_weight, preferred_element_type=jnp.float32) + mid_bias
        ).astype(jnp.bfloat16)
        partial_value = jnp.dot(second_hidden, stacked_out, preferred_element_type=jnp.float32)
        below_part = partial_value[:, 0:NVAR].reshape(block_size, FEAT)
        centre_part = partial_value[:, NVAR : 2 * NVAR].reshape(block_size, FEAT)
        above_part = partial_value[:, 2 * NVAR : 3 * NVAR].reshape(block_size, FEAT)
        zero_edge = jnp.zeros((block_size, NVAR), jnp.float32)
        from_below = jnp.concatenate([zero_edge, below_part[:, :-NVAR]], axis=1)
        from_above = jnp.concatenate([above_part[:, NVAR:], zero_edge], axis=1)
        result = from_below + centre_part + from_above
        return result.astype(jnp.bfloat16)

    outputs = lax.map(one_block, packets.reshape(count // block_size, block_size, FEAT))
    return outputs.reshape(count, FEAT)


def shards(model_state, send_slots, in_weight, in_bias, mid_weight, mid_bias, out_weight):
    lat_rows, lon_cols, features = model_state.shape
    column_count = lat_rows * lon_cols
    peers = send_slots.shape[2]
    per_pair = send_slots.shape[3]
    slot_list = send_slots.reshape(peers * per_pair)
    is_live = slot_list >= 0
    columns = model_state.reshape(column_count, features)
    lon_ext = with_halo(model_state, (("lon", 1),), 1, True)
    lat_ext = with_halo(model_state.astype(jnp.bfloat16), (("lat", 0),), 1, False).astype(
        model_state.dtype
    )
    lon_flux = face_flux(lon_ext[:, :-1], lon_ext[:, 1:], 0)
    lat_flux = face_flux(lat_ext[:-1], lat_ext[1:], 1)
    advection = -courant * (lon_flux[:, 1:] - lon_flux[:, :-1] + (lat_flux[1:] - lat_flux[:-1]))
    packets = jnp.take(columns, jnp.where(is_live, slot_list, 0), axis=0).astype(jnp.bfloat16)
    packets = jnp.where(is_live[:, None], packets, jnp.zeros_like(packets))
    received = lax.all_to_all(
        packets.reshape(peers, per_pair, features), "lon", split_axis=0, concat_axis=0, tiled=True
    )
    received_ids = lax.all_to_all(
        send_slots.reshape(peers, per_pair), "lon", split_axis=0, concat_axis=0, tiled=True
    )
    got_live = received_ids.reshape(peers * per_pair) >= 0
    position = jnp.cumsum(got_live.astype(jnp.int32)) - 1
    owned = peers * per_pair // 2
    selector = (position[None, :] == jnp.arange(owned, dtype=jnp.int32)[:, None]) & got_live[
        None, :
    ]
    selector = selector.astype(jnp.bfloat16)
    compact = jnp.dot(
        selector, received.reshape(peers * per_pair, features), preferred_element_type=jnp.float32
    ).astype(jnp.bfloat16)
    local_tend = column_physics(compact, in_weight, in_bias, mid_weight, mid_bias, out_weight)
    outgoing = jnp.dot(selector.T, local_tend, preferred_element_type=jnp.float32).astype(
        jnp.bfloat16
    )
    returned = lax.all_to_all(
        outgoing.reshape(peers, per_pair, features), "lon", split_axis=0, concat_axis=0, tiled=True
    )
    tendency = returned.reshape(peers * per_pair, features)
    target = jnp.where(is_live, slot_list, column_count)
    field = (
        jnp.zeros((column_count, features), jnp.float32)
        .at[target]
        .add(tendency.astype(jnp.float32), mode="drop")
    )
    physics_field = field.reshape(lat_rows, lon_cols, features)
    return model_state + advection + phys_weight * physics_field


def solution(mesh):
    return jax.shard_map(
        shards,
        mesh=mesh,
        in_specs=(P("lat", "lon", None), P("lat", "lon", None, None), P(), P(), P(), P(), P()),
        out_specs=P("lat", "lon", None),
        check_vma=False,
    )
```

profile of v0, /device:TPU:14, one launch (start us, length us, event | category | flops | bytes accessed | tf_op | source)
XLA Modules:
  0.0 173.9 jit_solution(923296572422148841)
XLA Ops:
  0.0 1.4 copy.63
  1.4 20.0 %all-to-all-start = ((s32[32,1,4]{2,1,0:T(1,128)}), s32[32,1,4]{2,1,0:T(1,128)S(1)}, u32[]{:S(2)}, u32[]{:S(2)}) async-start(s32[32,1,4]{2,1,0:T(1,128)} %copy.63), calls=%async_computation | async-start | bytes 32768 | tf_op jit(solution)/shard_map/all_to_all | solution.py:88
  21.5 1.3 constant_dynamic-update-slice_fusion
  22.8 3.3 %collective-permute-start.3 = (bf16[1,16,960]{2,1,0:T(8,128)(2,1)S(1)}, bf16[1,16,960]{2,1,0:T(8,128)(2,1)S(1)}, u32[]{:S(2)}, u32[]{:S(2)}) collective-permute-start(bf16[1,16,960]{2,1,0:T(8,128)(2,1)S(1)} %get-tuple-element.39), channel_id=1, source_target_pairs={{32,0},{64,32},{96,64},{128,96},{160,128},{192,160},{224,192},{256... | collective-permute-start | bytes 92168 | tf_op jit(solution)/shard_map/ppermute | solution.py:26
  26.2 4.6 %collective-permute-start.2 = (bf16[1,16,960]{2,1,0:T(8,128)(2,1)S(1)}, bf16[1,16,960]{2,1,0:T(8,128)(2,1)S(1)}, u32[]{:S(2)}, u32[]{:S(2)}) collective-permute-start(bf16[1,16,960]{2,1,0:T(8,128)(2,1)S(1)} %get-tuple-element.38), channel_id=1, source_target_pairs={{0,32},{32,64},{64,96},{96,128},{128,160},{160,192},{192,224},{224... | collective-permute-start | bytes 92168 | tf_op jit(solution)/shard_map/ppermute | solution.py:25
  30.8 1.1 fusion.31
  31.9 9.0 %collective-permute-start.1 = (f32[8,1,960]{2,1,0:T(1,128)S(1)}, f32[8,1,960]{2,1,0:T(1,128)S(1)}, u32[]{:S(2)}, u32[]{:S(2)}) collective-permute-start(f32[8,1,960]{2,1,0:T(1,128)S(1)} %get-tuple-element.34), channel_id=1, source_target_pairs={{1,0},{2,1},{3,2},{4,3},{5,4},{6,5},{7,6},{8,7},{9,8},{10,9},{11,1... | collective-permute-start | bytes 92168 | tf_op jit(solution)/shard_map/ppermute | solution.py:26
  40.9 1.9 %collective-permute-start = (f32[8,1,960]{2,1,0:T(1,128)S(1)}, f32[8,1,960]{2,1,0:T(1,128)S(1)}, u32[]{:S(2)}, u32[]{:S(2)}) collective-permute-start(f32[8,1,960]{2,1,0:T(1,128)S(1)} %get-tuple-element.32), channel_id=1, source_target_pairs={{0,1},{1,2},{2,3},{3,4},{4,5},{5,6},{6,7},{7,8},{8,9},{9,10},{10,1... | collective-permute-start | bytes 92168 | tf_op jit(solution)/shard_map/ppermute | solution.py:25
  42.8 0.8 copy.62
  43.5 0.7 bitcast_compare_fusion
  44.4 2.1 %gather_fusion = bf16[128,960]{1,0:T(8,128)(2,1)S(1)} fusion(f32[128,960]{1,0:T(8,128)} %bitcast.42, s32[1024]{0:T(1024)S(1)} %pad_clamp_fusion), kind=kCustom, calls=%fused_computation | custom fusion | bytes 492032 | tf_op jit(solution)/shard_map/jit(_take)/gather | solution.py:83
  46.8 1.0 fusion.6
  47.8 9.4 %all-to-all-start.1 = ((bf16[32,4,960]{2,1,0:T(4,128)(2,1)}), bf16[32,4,960]{2,1,0:T(4,128)(2,1)S(1)}, u32[]{:S(2)}, u32[]{:S(2)}) async-start(bf16[32,4,960]{2,1,0:T(4,128)(2,1)} %fusion.6), calls=%async_computation.1 | async-start | bytes 524288 | tf_op jit(solution)/shard_map/all_to_all | solution.py:85
  57.9 1.0 fusion.30
  58.9 2.3 %slice.97 = f32[9,16,60]{2,1,0:T(8,128)S(1)} slice(f32[9,16,960]{2,1,0:T(8,128)} %get-tuple-element.23), slice={[0:9:1], [0:16:1], [1:960:16]} | slice | bytes 69120 | tf_op jit(solution)/shard_map/slice | solution.py:32
  61.1 1.2 slice.99
  62.4 1.0 pad_maximum_fusion
  63.4 3.3 %broadcast_in_dim.57 = f32[9,16,60,16]{3,2,1,0:T(8,128)} broadcast(f32[9,16,60]{2,1,0:T(8,128)S(1)} %get-tuple-element.43), dimensions={0,1,2} | broadcast | bytes 587520 | tf_op jit(solution)/shard_map/broadcast_in_dim | solution.py:34
  66.7 4.7 %min.17 = f32[9,16,960]{2,1,0:T(8,128)S(1)} reshape(f32[9,16,60,16]{3,2,1,0:T(8,128)} %broadcast_in_dim.57) | data formatting | bytes 1105920 | tf_op jit(solution)/shard_map/min | solution.py:35
  71.4 3.3 %broadcast_in_dim.56 = f32[9,16,60,16]{3,2,1,0:T(8,128)} broadcast(f32[9,16,60]{2,1,0:T(8,128)S(1)} %get-tuple-element.42), dimensions={0,1,2} | broadcast | bytes 587520 | tf_op jit(solution)/shard_map/broadcast_in_dim | solution.py:34
  74.7 5.3 %max.17 = f32[9,16,960]{2,1,0:T(8,128)} reshape(f32[9,16,60,16]{3,2,1,0:T(8,128)} %broadcast_in_dim.56) | data formatting | bytes 1105920 | tf_op jit(solution)/shard_map/max | solution.py:35
  80.0 2.3 %slice.89 = f32[8,17,60]{2,1,0:T(8,128)S(1)} slice(f32[8,17,960]{2,1,0:T(8,128)} %pad_maximum_fusion), slice={[0:8:1], [0:17:1], [0:960:16]} | slice | bytes 65280 | tf_op jit(solution)/shard_map/slice | solution.py:32
  82.7 1.2 slice.91
  83.9 2.8 %broadcast_in_dim.55 = f32[8,17,60,16]{3,2,0,1:T(8,128)} broadcast(f32[8,17,60]{2,0,1:T(8,128)S(1)} %copy.60), dimensions={0,1,2} | broadcast | bytes 554880 | tf_op jit(solution)/shard_map/broadcast_in_dim | solution.py:34
  86.7 5.2 %min.15 = f32[8,17,960]{2,0,1:T(8,128)} reshape(f32[8,17,60,16]{3,2,0,1:T(8,128)} %broadcast_in_dim.55) | data formatting | bytes 1044480 | tf_op jit(solution)/shard_map/min | solution.py:35
  91.9 2.8 %broadcast_in_dim.54 = f32[8,17,60,16]{3,2,0,1:T(8,128)} broadcast(f32[8,17,60]{2,0,1:T(8,128)S(1)} %copy.58), dimensions={0,1,2} | broadcast | bytes 554880 | tf_op jit(solution)/shard_map/broadcast_in_dim | solution.py:34
  94.7 5.2 %max.15 = f32[8,17,960]{2,0,1:T(8,128)} reshape(f32[8,17,60,16]{3,2,0,1:T(8,128)} %broadcast_in_dim.54) | data formatting | bytes 1044480 | tf_op jit(solution)/shard_map/max | solution.py:35
  100.2 0.8 pad_slice_fusion
  101.5 2.5 %reshape.193 = bf16[3840,16]{1,0:T(8,128)(2,1)} reshape(bf16[64,960]{1,0:T(8,128)(2,1)} %get-tuple-element.45) | data formatting | bytes 245760 | tf_op jit(solution)/shard_map/while/body/eval_jaxpr/reshape | solution.py:48
  104.0 4.8 %fusion.16 = f32[3840,406]{0,1:T(8,128)} fusion(bf16[3840,16]{1,0:T(8,128)(2,1)} %reshape.193, bf16[3,16,406]{2,1,0:T(8,128)(2,1)S(1)} %copy-done.5), kind=kOutput, calls=%fused_computation.42 | convolution fusion | flops 49889280 | bytes 6375424 | tf_op jit(solution)/shard_map/while/body/eval_jaxpr/dot_general | solution.py:49
  108.9 3.6 %fusion.14 = f32[3840,406]{0,1:T(8,128)} fusion(bf16[3840,16]{1,0:T(8,128)(2,1)S(1)} %reshape.194, bf16[3,16,406]{2,1,0:T(8,128)(2,1)S(1)} %copy-done.5), kind=kOutput, calls=%fused_computation.40 | convolution fusion | flops 49889280 | bytes 7235584 | tf_op jit(solution)/shard_map/while/body/eval_jaxpr/dot_general | solution.py:49
  113.0 7.0 %multiply_convert_fusion.1 = bf16[3840,406]{0,1:T(8,128)(2,1)} fusion(f32[3840,406]{0,1:T(8,128)} %fusion.16, f32[3840,406]{0,1:T(8,128)} %fusion.14, bf16[3840,16]{1,0:T(8,128)(2,1)S(1)} %reshape.195, f32[406]{0:T(512)S(1)} %copy-done.7, bf16[3,16,406]{2,1,0:T(8,128)(2,1)S(1)} %copy-done.5), kind=kOutput, calls=%fused_computation.3 | convolution fusion | flops 62361600 | bytes 16591872 | tf_op jit(solution)/shard_map/while/body/eval_jaxpr/dot_general | solution.py:49
  120.0 5.9 %fusion = f32[3840,48]{0,1:T(8,128)} fusion(bf16[406,48]{0,1:T(8,128)(2,1)S(1)} %bitcast.46, bf16[3840,406]{0,1:T(8,128)(2,1)} %multiply_convert_fusion.1, bf16[406,406]{1,0:T(8,128)(2,1)S(1)} %copy-done, f32[406]{0:T(512)S(1)} %copy-done.8), kind=kOutput, calls=%fused_computation.4 | convolution fusion | flops 1424962560 | bytes 4225632 | tf_op jit(solution)/shard_map/while/body/eval_jaxpr/dot_general | solution.py:54
  125.9 1.2 fusion.29
  127.1 1.9 %copy.69 = f32[3840,16]{1,0:T(8,128)} copy(f32[3840,16]{0,1:T(8,128)S(1)} %get-tuple-element.20) | data formatting | bytes 491520 | tf_op jit(solution)/shard_map/while/body/eval_jaxpr/slice | solution.py:57
  128.9 2.1 %reshape.199 = f32[64,960]{1,0:T(8,128)S(1)} reshape(f32[3840,16]{1,0:T(8,128)} %copy.69) | data formatting | bytes 491520 | tf_op jit(solution)/shard_map/while/body/eval_jaxpr/reshape | solution.py:57
  131.2 1.9 %copy.68 = f32[3840,16]{1,0:T(8,128)} copy(f32[3840,16]{0,1:T(8,128)S(1)} %get-tuple-element.21) | data formatting | bytes 491520 | tf_op jit(solution)/shard_map/while/body/eval_jaxpr/slice | solution.py:56
  133.0 2.1 %reshape.198 = f32[64,960]{1,0:T(8,128)S(1)} reshape(f32[3840,16]{1,0:T(8,128)} %copy.68) | data formatting | bytes 491520 | tf_op jit(solution)/shard_map/while/body/eval_jaxpr/reshape | solution.py:56
  135.1 1.9 %copy.67 = f32[3840,16]{1,0:T(8,128)} copy(f32[3840,16]{0,1:T(8,128)S(1)} %get-tuple-element.19) | data formatting | bytes 491520 | tf_op jit(solution)/shard_map/while/body/eval_jaxpr/slice | solution.py:55
  137.0 2.1 %reshape.197 = f32[64,960]{1,0:T(8,128)S(1)} reshape(f32[3840,16]{1,0:T(8,128)} %copy.67) | data formatting | bytes 491520 | tf_op jit(solution)/shard_map/while/body/eval_jaxpr/reshape | solution.py:55
  139.6 0.8 reshape.200
  140.5 12.2 %all-to-all-start.2 = ((bf16[32,4,960]{2,1,0:T(4,128)(2,1)}), bf16[32,4,960]{2,1,0:T(4,128)(2,1)S(1)}, u32[]{:S(2)}, u32[]{:S(2)}) async-start(bf16[32,4,960]{2,1,0:T(4,128)(2,1)} %reshape.200), calls=%async_computation.2 | async-start | bytes 524288 | tf_op jit(solution)/shard_map/all_to_all | solution.py:105
  152.7 1.2 multiply_add_fusion
  153.9 2.2 %fusion.1 = f32[8,17,960]{2,1,0:T(8,128)S(1)} fusion(f32[8,17,960]{2,1,0:T(8,128)} %copy-done.2, f32[8,17,960]{2,0,1:T(8,128)} %min.15, f32[8,17,960]{2,0,1:T(8,128)} %max.15, f32[8,16,960]{2,1,0:T(8,128)S(1)} %copy-done.1, f32[8,1,960]{2,1,0:T(1,128)S(1)} %copy-done.4), kind=kLoop, calls=%fused_computation.9 | loop fusion | flops 522240 | bytes 2611200 | tf_op jit(solution)/shard_map/add | solution.py:35
  156.2 13.6 %all-to-all-done.2 = bf16[32,4,960]{2,1,0:T(4,128)(2,1)S(1)} async-done(((bf16[32,4,960]{2,1,0:T(4,128)(2,1)}), bf16[32,4,960]{2,1,0:T(4,128)(2,1)S(1)}, u32[]{:S(2)}, u32[]{:S(2)}) %all-to-all-start.2) | async-done | bytes 245792 | tf_op jit(solution)/shard_map/all_to_all | solution.py:105
  169.7 0.9 reshape.215
  170.6 2.2 %scatter_custom_fusion = f32[128,960]{1,0:T(8,128)S(1)} fusion(s32[128]{0:T(128)S(1)} %get-tuple-element.49, f32[128,960]{1,0:T(8,128)} %reshape.215, f32[]{:T(128)} %constant.19.clone.1), kind=kCustom, calls=%fused_computation.23 | custom fusion | flops 122880 | bytes 492032 | tf_op jit(solution)/shard_map/scatter-add | solution.py:113
  172.9 1.0 fusion.5
  (51 shorter events, 3.5 us)
Async XLA Ops:
  0.0 120.0 %copy-start = (bf16[406,406]{1,0:T(8,128)(2,1)S(1)}, bf16[406,406]{1,0:T(8,128)(2,1)}, u32[]{:S(2)}) copy-start(bf16[406,406]{1,0:T(8,128)(2,1)} %param.11) | copy-start | bytes 989020
  0.0 62.4 %copy-start.1 = (f32[8,16,960]{2,1,0:T(8,128)S(1)}, f32[8,16,960]{2,1,0:T(8,128)}, u32[]{:S(2)}) copy-start(f32[8,16,960]{2,1,0:T(8,128)} %param.7) | copy-start | bytes 1474564
  1.4 46.3 %all-to-all-start = ((s32[32,1,4]{2,1,0:T(1,128)}), s32[32,1,4]{2,1,0:T(1,128)S(1)}, u32[]{:S(2)}, u32[]{:S(2)}) async-start(s32[32,1,4]{2,1,0:T(1,128)} %copy.63), calls=%async_computation | async-start | bytes 32768 | tf_op jit(solution)/shard_map/all_to_all | solution.py:88
  22.8 35.0 %collective-permute-start.3 = (bf16[1,16,960]{2,1,0:T(8,128)(2,1)S(1)}, bf16[1,16,960]{2,1,0:T(8,128)(2,1)S(1)}, u32[]{:S(2)}, u32[]{:S(2)}) collective-permute-start(bf16[1,16,960]{2,1,0:T(8,128)(2,1)S(1)} %get-tuple-element.39), channel_id=1, source_target_pairs={{32,0},{64,32},{96,64},{128,96},{160,128},{192,160},{224,192},{256... | collective-permute-start | bytes 92168 | tf_op jit(solution)/shard_map/ppermute | solution.py:26
  26.2 31.6 %collective-permute-start.2 = (bf16[1,16,960]{2,1,0:T(8,128)(2,1)S(1)}, bf16[1,16,960]{2,1,0:T(8,128)(2,1)S(1)}, u32[]{:S(2)}, u32[]{:S(2)}) collective-permute-start(bf16[1,16,960]{2,1,0:T(8,128)(2,1)S(1)} %get-tuple-element.38), channel_id=1, source_target_pairs={{0,32},{32,64},{64,96},{96,128},{128,160},{160,192},{192,224},{224... | collective-permute-start | bytes 92168 | tf_op jit(solution)/shard_map/ppermute | solution.py:25
  31.9 50.4 %collective-permute-start.1 = (f32[8,1,960]{2,1,0:T(1,128)S(1)}, f32[8,1,960]{2,1,0:T(1,128)S(1)}, u32[]{:S(2)}, u32[]{:S(2)}) collective-permute-start(f32[8,1,960]{2,1,0:T(1,128)S(1)} %get-tuple-element.34), channel_id=1, source_target_pairs={{1,0},{2,1},{3,2},{4,3},{5,4},{6,5},{7,6},{8,7},{9,8},{10,9},{11,1... | collective-permute-start | bytes 92168 | tf_op jit(solution)/shard_map/ppermute | solution.py:26
  40.9 21.5 %collective-permute-start = (f32[8,1,960]{2,1,0:T(1,128)S(1)}, f32[8,1,960]{2,1,0:T(1,128)S(1)}, u32[]{:S(2)}, u32[]{:S(2)}) collective-permute-start(f32[8,1,960]{2,1,0:T(1,128)S(1)} %get-tuple-element.32), channel_id=1, source_target_pairs={{0,1},{1,2},{2,3},{3,4},{4,5},{5,6},{6,7},{7,8},{8,9},{9,10},{10,1... | collective-permute-start | bytes 92168 | tf_op jit(solution)/shard_map/ppermute | solution.py:25
  47.8 52.2 %all-to-all-start.1 = ((bf16[32,4,960]{2,1,0:T(4,128)(2,1)}), bf16[32,4,960]{2,1,0:T(4,128)(2,1)S(1)}, u32[]{:S(2)}, u32[]{:S(2)}) async-start(bf16[32,4,960]{2,1,0:T(4,128)(2,1)} %fusion.6), calls=%async_computation.1 | async-start | bytes 524288 | tf_op jit(solution)/shard_map/all_to_all | solution.py:85
  62.4 1.0 copy-start.3
  82.6 12.1 %copy-start.2 = (f32[8,17,960]{2,1,0:T(8,128)}, f32[8,17,960]{2,1,0:T(8,128)S(1)}, u32[]{:S(2)}) copy-start(f32[8,17,960]{2,1,0:T(8,128)S(1)} %dynamic-update-slice.1) | copy-start | bytes 1566724
  91.9 12.1 %copy-start.5 = (bf16[3,16,406]{2,1,0:T(8,128)(2,1)S(1)}, bf16[3,16,406]{2,1,0:T(8,128)(2,1)}, u32[]{:S(2)}) copy-start(bf16[3,16,406]{2,1,0:T(8,128)(2,1)} %param.9) | copy-start | bytes 116932
  108.9 4.1 %copy-start.7 = (f32[406]{0:T(512)S(1)}, f32[406]{0:T(512)}, u32[]{:S(2)}) copy-start(f32[406]{0:T(512)} %param.10) | copy-start | bytes 4876
  113.0 7.0 %copy-start.6 = (bf16[3,406,16]{1,2,0:T(8,128)(2,1)S(1)}, bf16[3,406,16]{1,2,0:T(8,128)(2,1)}, u32[]{:S(2)}) copy-start(bf16[3,406,16]{1,2,0:T(8,128)(2,1)} %param.13) | copy-start | bytes 116932
  113.0 7.0 %copy-start.8 = (f32[406]{0:T(512)S(1)}, f32[406]{0:T(512)}, u32[]{:S(2)}) copy-start(f32[406]{0:T(512)} %param.12) | copy-start | bytes 4876
  133.0 20.9 %copy-start.4 = (f32[8,1,960]{2,1,0:T(1,128)S(1)}, f32[8,1,960]{2,1,0:T(1,128)}, u32[]{:S(2)}) copy-start(f32[8,1,960]{2,1,0:T(1,128)} %copy-done.3) | copy-start | bytes 92164
  140.5 29.3 %all-to-all-start.2 = ((bf16[32,4,960]{2,1,0:T(4,128)(2,1)}), bf16[32,4,960]{2,1,0:T(4,128)(2,1)S(1)}, u32[]{:S(2)}, u32[]{:S(2)}) async-start(bf16[32,4,960]{2,1,0:T(4,128)(2,1)} %reshape.200), calls=%async_computation.2 | async-start | bytes 524288 | tf_op jit(solution)/shard_map/all_to_all | solution.py:105
where the time goes:
time: 175 us; the launch traced here: 174 us
  local copies, waits for them, and re-layouts  66.2 us (38%)
  starting transfers between devices  60.5 us (35%)
  matrix products  21.9 us (13%)
  waiting for transfers between devices  13.6 us (8%)
  other arithmetic  11.3 us (6%)
    all_to_all x1, starting transfers between devices, shards(): lax.all_to_all(send_slots.reshape(peers, per_pair), 'lon', split_axis=0,...  20 us
    dot_general x3, matrix products, one_block(): jnp.dot(window, in_weight[tap], preferred_element_type=jnp.float32)  15.5 us
    all_to_all x1, waiting for transfers between devices, shards(): lax.all_to_all(outgoing.reshape(peers, per_pair, features), 'lon', split_...  13.6 us
    ppermute x2, starting transfers between devices, with_halo(): after = lax.ppermute(first, axis, down)  12.3 us
    all_to_all x1, starting transfers between devices, shards(): lax.all_to_all(outgoing.reshape(peers, per_pair, features), 'lon', split_...  12.2 us
    broadcast_in_dim x4, local copies, waits for them, and re-layouts, face_flux(): speed = jnp.repeat(0.5 * (wind_low + wind_high), NVAR, axis=-1)  12.1 us
    max x3, local copies, waits for them, and re-layouts, face_flux(): return jnp.maximum(speed, 0.0) * lower + jnp.minimum(speed, 0.0) * upper  10.6 us
    min x3, local copies, waits for them, and re-layouts, face_flux(): return jnp.maximum(speed, 0.0) * lower + jnp.minimum(speed, 0.0) * upper  9.94 us
  transfers between devices with their start and end apart: 7, of which 1 were waited for; matrix products, arithmetic and copies ran while one was open for 31% of the time, Pallas kernels for 0%

commit v1 on v0

v1 whole, which is shorter than its diff:
```python
import functools

import jax
import jax.numpy as jnp
from jax import lax
from jax.experimental import pallas as pl
from jax.experimental.pallas import tpu as pltpu
from jax.sharding import PartitionSpec as P

MESH = pl.DeviceIdType.MESH

LEV = 60
NVAR = 16
HID = 406
HPAD = 416
FEAT = 960
ROWS = 8
COLS = 16
CELLS = ROWS * COLS
LANES = 128
CHUNK = 4

courant = 0.1


def split3(x):
    hi = x.astype(jnp.bfloat16).astype(jnp.float32)
    mid = (x - hi).astype(jnp.bfloat16).astype(jnp.float32)
    lo = (x - hi) - mid
    return hi, mid, lo


def bias_rows(block, bias, first):
    row = lax.broadcasted_iota(jnp.int32, block.shape, 0)
    for n, part in enumerate(split3(bias)):
        block = jnp.where(row == first + n, part, block)
    return block


def swish(y):
    return (y + y * jnp.tanh(y)).astype(jnp.bfloat16)


def spread(x, component):
    lane = lax.broadcasted_iota(jnp.int32, (x.shape[0], LANES), 1)
    source = (lane // NVAR) * NVAR + component
    parts = []
    for start in range(0, FEAT, LANES):
        width = min(LANES, FEAT - start)
        part = x[:, start : start + width]
        if width < LANES:
            part = jnp.concatenate([part, jnp.zeros((x.shape[0], LANES - width), x.dtype)], axis=1)
        parts.append(jnp.take_along_axis(part, source, axis=1)[:, :width])
    return jnp.concatenate(parts, axis=1)


def flux(lower, upper, component):
    speed = spread(lower + upper, component)
    return jnp.maximum(speed, 0.0) * lower + jnp.minimum(speed, 0.0) * upper


def kernel(
    n_lat, n_lon,
    state, slots, w1, b1, wm, bm, wo, out,
    own, xt, a1, am, w1t, wmt, wot, brow, p0, p1, p2, h1, h2, result,
    edge_w, edge_e, halo_w, halo_e, halo_s, halo_n,
    load_sem, store_sem, send_sem, recv_sem,
):
    lat, lon = lax.axis_index("lat"), lax.axis_index("lon")
    east, west = lax.rem(lon + 1, n_lon), lax.rem(lon + n_lon - 1, n_lon)
    has_south, has_north = lat > 0, lat < n_lat - 1
    barrier = pltpu.get_barrier_semaphore()

    def greet(a, b):
        pl.semaphore_signal(barrier, inc=1, device_id=(a, b), device_id_type=MESH)

    greet(lat, east)
    greet(lat, west)
    pl.when(has_south)(lambda: greet(lat - 1, lon))
    pl.when(has_north)(lambda: greet(lat + 1, lon))

    load = pltpu.make_async_copy(state, own, load_sem)
    load.start()

    brow[...] = jnp.zeros_like(brow)
    brow[0:1, 0:HID] = b1[...].reshape(1, HID) * 0.5
    brow[1:2, 0:HID] = bm[...].reshape(1, HID) * 0.5
    a1[...] = jnp.zeros_like(a1)
    a1[0:48, 0:HID] = w1[...] * jnp.bfloat16(0.5)
    a1[48:64, :] = bias_rows(jnp.zeros((16, 512), jnp.float32), brow[0:1, :], 0).astype(jnp.bfloat16)
    w1t[...] = jnp.transpose(a1[...], (1, 0))
    am[...] = jnp.zeros_like(am)
    am[0:HID, 0:HID] = wm[...] * jnp.bfloat16(0.5)
    am[400:416, :] = bias_rows(am[400:416, :].astype(jnp.float32), brow[1:2, :], 6).astype(jnp.bfloat16)
    wmt[...] = jnp.transpose(am[...], (1, 0))
    wot[...] = jnp.zeros_like(wot)
    for k in range(3):
        wot[16 * k : 16 * k + 16, 0:HID] = wo[k] * jnp.bfloat16(0.5)

    load.wait()
    edge_w[...] = own[:, 0, :]
    edge_e[...] = own[:, COLS - 1, :]
    cells = own[...].reshape(CELLS, FEAT).astype(jnp.bfloat16)
    xt[0:16, :] = jnp.zeros((16, LANES), jnp.bfloat16)
    xt[16 + FEAT :, :] = jnp.zeros((16, LANES), jnp.bfloat16)
    for start in range(0, FEAT, LANES):
        width = min(LANES, FEAT - start)
        xt[16 + start : 16 + start + width, :] = jnp.transpose(cells[:, start : start + width], (1, 0))

    p0[...] = jnp.zeros_like(p0)
    p1[...] = jnp.zeros_like(p1)
    p2[...] = jnp.zeros_like(p2)
    ones = jnp.ones((16, LANES), jnp.bfloat16)
    last_row = lax.broadcasted_iota(jnp.int32, (16, CHUNK * LANES), 0)
    is_one = (last_row >= 6) & (last_row < 9)

    def physics(step, carry):
        level = step * CHUNK
        windows = []
        for j in range(CHUNK):
            start = pl.multiple_of((level + j) * 16, 16)
            windows.append(jnp.concatenate([xt[pl.ds(start, 48), :], ones], axis=0))
        window = jnp.concatenate(windows, axis=1)
        first = swish(jnp.dot(w1t[0:HPAD, :], window, preferred_element_type=jnp.float32))
        h1[0:400, :] = first[0:400]
        h1[400:416, :] = jnp.where(is_one, jnp.bfloat16(1.0), first[400:416])
        h2[...] = swish(jnp.dot(wmt[0:HPAD, 0:HPAD], h1[...], preferred_element_type=jnp.float32))
        part = jnp.dot(wot[:, 0:HPAD], h2[...], preferred_element_type=jnp.float32)
        for j in range(CHUNK):
            start = pl.multiple_of((level + j) * 16, 16)
            lanes = slice(LANES * j, LANES * (j + 1))
            p0[pl.ds(start + 32, 16), :] = part[0:16, lanes]
            p1[pl.ds(start + 16, 16), :] = part[16:32, lanes]
            p2[pl.ds(start, 16), :] = part[32:48, lanes]
        return carry

    early = 4
    lax.fori_loop(0, early, physics, 0)

    peers = 2 + has_south.astype(jnp.int32) + has_north.astype(jnp.int32)
    pl.semaphore_wait(barrier, peers)

    def copy(n, src, dst, a, b):
        return pltpu.make_async_remote_copy(
            src_ref=src, dst_ref=dst, send_sem=send_sem.at[n], recv_sem=recv_sem.at[n],
            device_id=(a, b), device_id_type=MESH,
        )

    to_east = copy(0, edge_e, halo_w, lat, east)
    to_west = copy(1, edge_w, halo_e, lat, west)
    to_north = copy(2, own.at[ROWS - 1], halo_s, lat + 1, lon)
    to_south = copy(3, own.at[0], halo_n, lat - 1, lon)
    to_east.start()
    to_west.start()
    pl.when(has_north)(lambda: to_north.start())
    pl.when(has_south)(lambda: to_south.start())

    lax.fori_loop(early, LEV // CHUNK, physics, 0)

    peers = slots.shape[1]
    column = lax.broadcasted_iota(jnp.int32, (LANES, peers), 0)
    hits = jnp.zeros((LANES, peers), jnp.float32)
    for s in range(slots.shape[0]):
        hits = jnp.where(slots[s : s + 1, :] == column, 1.0, hits)
    alive = jnp.max(hits, axis=1, keepdims=True)

    for start in range(0, FEAT, LANES):
        width = min(LANES, FEAT - start)
        rows = slice(16 + start, 16 + start + width)
        total = p0[rows, :] + p1[rows, :] + p2[rows, :]
        tend = jnp.transpose(total.astype(jnp.bfloat16), (1, 0)).astype(jnp.float32)
        tend = jnp.where(alive > 0.0, tend, 0.0)
        result[:, :, start : start + width] = own[:, :, start : start + width] + tend.reshape(
            ROWS, COLS, width
        )

    scale = -0.5 * courant
    for r in range(ROWS):
        centre = own[r]
        faces = flux(centre[:-1], centre[1:], 0)
        none = jnp.zeros((1, FEAT), jnp.float32)
        div = jnp.concatenate([faces, none], axis=0) - jnp.concatenate([none, faces], axis=0)
        result[r] = result[r] + scale * div
        if r < ROWS - 1:
            face = scale * flux(centre, own[r + 1], 1)
            result[r] = result[r] + face
            result[r + 1] = result[r + 1] - face

    pl.when(has_south)(lambda: to_north.wait_recv())
    pl.when(has_north)(lambda: to_south.wait_recv())
    south = jnp.where(has_south, halo_s[...], 0.0)
    north = jnp.where(has_north, halo_n[...], 0.0)
    result[0] = result[0] - scale * flux(south, own[0], 1)
    result[ROWS - 1] = result[ROWS - 1] + scale * flux(own[ROWS - 1], north, 1)
    to_east.wait_recv()
    to_west.wait_recv()
    result[:, 0, :] = result[:, 0, :] - scale * flux(halo_w[...], own[:, 0, :], 0)
    result[:, COLS - 1, :] = result[:, COLS - 1, :] + scale * flux(own[:, COLS - 1, :], halo_e[...], 0)

    store = pltpu.make_async_copy(result, out, store_sem)
    store.start()
    to_east.wait_send()
    to_west.wait_send()
    pl.when(has_north)(lambda: to_north.wait_send())
    pl.when(has_south)(lambda: to_south.wait_send())
    store.wait()


def shards(n_lat, n_lon, model_state, send_slots, in_weight, in_bias, mid_weight, mid_bias, out_weight):
    vmem = pl.BlockSpec(memory_space=pltpu.VMEM)
    hbm = pl.BlockSpec(memory_space=pl.ANY)
    f32, bf16 = jnp.float32, jnp.bfloat16
    return pl.pallas_call(
        functools.partial(kernel, n_lat, n_lon),
        out_shape=jax.ShapeDtypeStruct(model_state.shape, f32),
        in_specs=[hbm] + [vmem] * 6,
        out_specs=hbm,
        scratch_shapes=[
            pltpu.VMEM((ROWS, COLS, FEAT), f32),
            pltpu.VMEM((FEAT + 32, LANES), bf16),
            pltpu.VMEM((64, 512), bf16),
            pltpu.VMEM((512, 512), bf16),
            pltpu.VMEM((512, 64), bf16),
            pltpu.VMEM((512, 512), bf16),
            pltpu.VMEM((48, 512), bf16),
            pltpu.VMEM((8, 512), f32),
            pltpu.VMEM((FEAT + 32, LANES), f32),
            pltpu.VMEM((FEAT + 32, LANES), f32),
            pltpu.VMEM((FEAT + 32, LANES), f32),
            pltpu.VMEM((HPAD, CHUNK * LANES), bf16),
            pltpu.VMEM((HPAD, CHUNK * LANES), bf16),
            pltpu.VMEM((ROWS, COLS, FEAT), f32),
            pltpu.VMEM((ROWS, FEAT), f32),
            pltpu.VMEM((ROWS, FEAT), f32),
            pltpu.VMEM((ROWS, FEAT), f32),
            pltpu.VMEM((ROWS, FEAT), f32),
            pltpu.VMEM((COLS, FEAT), f32),
            pltpu.VMEM((COLS, FEAT), f32),
            pltpu.SemaphoreType.DMA,
            pltpu.SemaphoreType.DMA,
            pltpu.SemaphoreType.DMA((4,)),
            pltpu.SemaphoreType.DMA((4,)),
        ],
        compiler_params=pltpu.CompilerParams(collective_id=0, has_side_effects=True),
    )(
        model_state,
        jnp.transpose(send_slots.reshape(send_slots.shape[2:]), (1, 0)),
        in_weight.reshape(3 * NVAR, HID),
        in_bias,
        mid_weight,
        mid_bias,
        jnp.transpose(out_weight, (0, 2, 1)),
    )


def solution(mesh):
    return jax.shard_map(
        functools.partial(shards, mesh.shape["lat"], mesh.shape["lon"]),
        mesh=mesh,
        in_specs=(P("lat", "lon", None), P("lat", "lon", None, None), P(), P(), P(), P(), P()),
        out_specs=P("lat", "lon", None),
        check_vma=False,
    )
```

time: 175 us -> 29.4 us (0.17)
  local copies, waits for them, and re-layouts: 66.2 us -> 1.89 us
  starting transfers between devices: 60.5 us -> 0 us
  Pallas kernels: 0 us -> 27.2 us
  matrix products: 21.9 us -> 0 us
  waiting for transfers between devices: 13.6 us -> 0 us
  other arithmetic: 11.3 us -> 0 us
    all_to_all x3 -> x0, starting transfers between devices: 41.7 us -> none  [the longest x1 20 us: shards(): lax.all_to_all(send_slots.reshape(peers, per_pair), 'lon', split_axis=0,...]
    pallas_call x0 -> x1, Pallas kernels: none -> 27.2 us  [shards(): pl.pallas_call(functools.partial(kernel, n_lat, n_lon), out_shape=jax.Sha...]
    dot_general x6 -> x0, matrix products: 21.9 us -> none  [the longest x3 15.5 us: one_block(): jnp.dot(window, in_weight[tap], preferred_element_type=jnp.float32)]
    ppermute x4 -> x0, starting transfers between devices: 18.8 us -> none  [the longest x2 12.3 us: with_halo(): after = lax.ppermute(first, axis, down)]
    slice x13 -> x0, local copies, waits for them, and re-layouts: 16.8 us -> none  [the longest x2 4.55 us: face_flux(): wind_low = lower[..., component::NVAR]]
    all_to_all x3 -> x0, waiting for transfers between devices: 13.6 us -> none  [the longest x1 13.6 us: shards(): lax.all_to_all(outgoing.reshape(peers, per_pair, features), 'lon', split_...]
    broadcast_in_dim x4 -> x0, local copies, waits for them, and re-layouts: 12.1 us -> none  [face_flux(): speed = jnp.repeat(0.5 * (wind_low + wind_high), NVAR, axis=-1)]
    reshape x9 -> x0, local copies, waits for them, and re-layouts: 10.6 us -> none  [the longest x3 3.42 us: one_block(): padded[:, tap * NVAR:tap * NVAR + FEAT].reshape(block_size * LEV, NVAR)]
  transfers between devices with their start and end apart: 7 -> 0, of which waited for: 1 -> 0; matrix products, arithmetic and copies ran while one was open for 31% -> 0% of each run, Pallas kernels for 0% -> 0%
where the time goes in v1:
time: 29.4 us; the launch traced here: 29.1 us
  Pallas kernels  27.2 us (93%)
  local copies, waits for them, and re-layouts  1.89 us (6%)
    pallas_call x1, Pallas kernels, shards(): pl.pallas_call(functools.partial(kernel, n_lat, n_lon), out_shape=jax.Sha...  27.2 us
    unnamed x1, local copies, waits for them, and re-layouts  1.89 us

profile of v1, /device:TPU:14, one launch (start us, length us, event | category | flops | bytes accessed | tf_op | source)
XLA Modules:
  0.0 29.1 jit_solution(5965381838868787146)
XLA Ops:
  0.0 27.2 %shard_map.73 = f32[8,16,960]{2,1,0:T(8,128)} custom-call(f32[8,16,960]{2,1,0:T(8,128)} %state.1, s32[4,32]{1,0:T(4,128)} %bitcast.7, bf16[48,406]{1,0:T(8,128)(2,1)} %bitcast.5, f32[406]{0:T(512)} %b1.1, bf16[406,406]{1,0:T(8,128)(2,1)} %wm.1, f32[406]{0:T(512)} %bm.1, bf16[3,16,406]{2,1,0:T(8,128)(2,1)} %bitcast.6), custom_call_target="tpu_custom_call" | custom-call | tf_op jit(solution)/shard_map/pallas_call | solution.py:213
  27.3 1.9 %copy.9 = f32[8,16,960]{2,1,0:T(8,128)} copy(f32[8,16,960]{2,1,0:T(8,128)} %shard_map.73) | data formatting | bytes 983040

commit v2 on v1

v2 whole, which is shorter than its diff:
```python
import functools

import jax
import jax.numpy as jnp
from jax import lax
from jax.experimental import pallas as pl
from jax.experimental.pallas import tpu as pltpu
from jax.sharding import PartitionSpec as P

MESH = pl.DeviceIdType.MESH

LEV = 60
NVAR = 16
HID = 406
HPAD = 416
FEAT = 960
ROWS = 8
COLS = 16
CELLS = ROWS * COLS
LANES = 128
CHUNK = 4
VMEM_LIMIT = 66500000

courant = 0.1


def split3(x):
    hi = x.astype(jnp.bfloat16).astype(jnp.float32)
    mid = (x - hi).astype(jnp.bfloat16).astype(jnp.float32)
    lo = (x - hi) - mid
    return hi, mid, lo


def bias_rows(block, bias, first):
    row = lax.broadcasted_iota(jnp.int32, block.shape, 0)
    for n, part in enumerate(split3(bias)):
        block = jnp.where(row == first + n, part, block)
    return block


def swish(y):
    return (y + y * jnp.tanh(y)).astype(jnp.bfloat16)


def spread(x, component):
    lane = lax.broadcasted_iota(jnp.int32, (x.shape[0], LANES), 1)
    source = (lane // NVAR) * NVAR + component
    parts = []
    for start in range(0, FEAT, LANES):
        width = min(LANES, FEAT - start)
        part = x[:, start : start + width]
        if width < LANES:
            part = jnp.concatenate([part, jnp.zeros((x.shape[0], LANES - width), x.dtype)], axis=1)
        parts.append(jnp.take_along_axis(part, source, axis=1)[:, :width])
    return jnp.concatenate(parts, axis=1)


def flux(lower, upper, component):
    speed = spread(lower + upper, component)
    return jnp.maximum(speed, 0.0) * lower + jnp.minimum(speed, 0.0) * upper


EAST, WEST, NORTH, SOUTH = range(4)
OPPOSITE = (WEST, EAST, SOUTH, NORTH)


def neighbours(lat, lon, n_lat, n_lon):
    root = (lat == 0) & (lon == 0)
    half = n_lon // 2
    first_column, last_column = lon == 0, lon == n_lon - 1

    def lower_first(a):
        return (lax.rem(a, 8) < 4) | (lax.rem(a, 8) == 7)

    beside_root_e = (lat == 0) & last_column
    beside_root_w = (lat == 0) & (lon == 1)
    above_root = (lat == 1) & first_column
    has = (lon >= 0, lon >= 0, lat < n_lat - 1, lat > 0)
    first = (
        root | (last_column & (lat > 0)),
        root | ((lon > 0) & jnp.logical_not(beside_root_w)),
        root | jnp.logical_not(lower_first(lat)),
        lower_first(lat + 7) & jnp.logical_not(above_root),
    )
    far = (
        jnp.logical_not(first[EAST]) & ((lon == half - 1) | beside_root_e),
        jnp.logical_not(first[WEST]) & (first_column | beside_root_w),
        lat < 0,
        above_root,
    )
    return has, first, far


def kernel(
    n_lat, n_lon,
    state, slots_hbm, w1_hbm, b1_hbm, wm_hbm, bm_hbm, wo_hbm, out,
    own, slots, w1, b1, wm, bm, wo,
    xt, a1, am, w1t, wmt, wot, brow, p0, p1, p2, h1, h2,
    halo_e, halo_w, halo_n, halo_s,
    load_sem, send_sem, recv_sem, ready_sem,
):
    lat, lon = lax.axis_index("lat"), lax.axis_index("lon")
    has, first, far = neighbours(lat, lon, n_lat, n_lon)
    late = [jnp.logical_not(f) for f in first]
    near = [jnp.logical_not(f) for f in far]
    where = (
        (lat, lax.rem(lon + 1, n_lon)),
        (lat, lax.rem(lon + n_lon - 1, n_lon)),
        (lat + 1, lon),
        (lat - 1, lon),
    )
    barrier = pltpu.get_barrier_semaphore()

    def signal(sem, d):
        pl.semaphore_signal(sem, inc=1, device_id=where[d], device_id_type=MESH)

    for d in range(4):
        pl.when(has[d] & late[d])(functools.partial(signal, barrier, d))

    pairs = ((state, own), (w1_hbm, w1), (b1_hbm, b1), (bm_hbm, bm), (wm_hbm, wm), (wo_hbm, wo), (slots_hbm, slots))
    loads = [pltpu.make_async_copy(src, dst, load_sem.at[n]) for n, (src, dst) in enumerate(pairs)]
    for load in loads:
        load.start()

    halos = (halo_e, halo_w, halo_n, halo_s)
    edges = (state.at[:, COLS - 1, :], state.at[:, 0, :], state.at[ROWS - 1], state.at[0])
    sends = [
        pltpu.make_async_remote_copy(
            src_ref=edges[d], dst_ref=halos[OPPOSITE[d]], send_sem=send_sem.at[d], recv_sem=recv_sem.at[OPPOSITE[d]],
            device_id=where[d], device_id_type=MESH,
        )
        for d in range(4)
    ]
    count = jnp.int32(0)
    for d in range(4):
        count = count + (has[d] & first[d]).astype(jnp.int32)
    pl.when(count > 0)(lambda: pl.semaphore_wait(barrier, count))
    for d in range(4):

        @pl.when(has[d] & first[d])
        def _(d=d):
            sends[d].start()
            signal(ready_sem.at[OPPOSITE[d]], d)

    def answer(d):
        pl.semaphore_wait(ready_sem.at[d], 1)
        sends[d].start()

    a1[...] = jnp.zeros_like(a1)
    am[...] = jnp.zeros_like(am)
    wot[...] = jnp.zeros_like(wot)
    brow[...] = jnp.zeros_like(brow)
    for load in loads[1:]:
        load.wait()
    brow[0:1, 0:HID] = b1[...].reshape(1, HID) * 0.5
    brow[1:2, 0:HID] = bm[...].reshape(1, HID) * 0.5
    a1[0:48, 0:HID] = w1[...] * jnp.bfloat16(0.5)
    a1[48:64, :] = bias_rows(jnp.zeros((16, 512), jnp.float32), brow[0:1, :], 0).astype(jnp.bfloat16)
    w1t[...] = jnp.transpose(a1[...], (1, 0))
    am[0:HID, 0:HID] = wm[...] * jnp.bfloat16(0.5)
    am[400:416, :] = bias_rows(am[400:416, :].astype(jnp.float32), brow[1:2, :], 6).astype(jnp.bfloat16)
    wmt[...] = jnp.transpose(am[...], (1, 0))
    for k in range(3):
        wot[16 * k : 16 * k + 16, 0:HID] = wo[k] * jnp.bfloat16(0.5)

    loads[0].wait()
    cells = own[...].reshape(CELLS, FEAT).astype(jnp.bfloat16)
    xt[0:16, :] = jnp.zeros((16, LANES), jnp.bfloat16)
    xt[16 + FEAT :, :] = jnp.zeros((16, LANES), jnp.bfloat16)
    for start in range(0, FEAT, LANES):
        width = min(LANES, FEAT - start)
        xt[16 + start : 16 + start + width, :] = jnp.transpose(cells[:, start : start + width], (1, 0))

    p0[...] = jnp.zeros_like(p0)
    p1[...] = jnp.zeros_like(p1)
    p2[...] = jnp.zeros_like(p2)
    ones = jnp.ones((16, LANES), jnp.bfloat16)
    last_row = lax.broadcasted_iota(jnp.int32, (16, CHUNK * LANES), 0)
    is_one = (last_row >= 6) & (last_row < 9)

    def physics(step, carry):
        level = step * CHUNK
        windows = []
        for j in range(CHUNK):
            start = pl.multiple_of((level + j) * 16, 16)
            windows.append(jnp.concatenate([xt[pl.ds(start, 48), :], ones], axis=0))
        window = jnp.concatenate(windows, axis=1)
        hidden = swish(jnp.dot(w1t[0:HPAD, :], window, preferred_element_type=jnp.float32))
        h1[0:400, :] = hidden[0:400]
        h1[400:416, :] = jnp.where(is_one, jnp.bfloat16(1.0), hidden[400:416])
        h2[...] = swish(jnp.dot(wmt[0:HPAD, 0:HPAD], h1[...], preferred_element_type=jnp.float32))
        part = jnp.dot(wot[:, 0:HPAD], h2[...], preferred_element_type=jnp.float32)
        for j in range(CHUNK):
            start = pl.multiple_of((level + j) * 16, 16)
            lanes = slice(LANES * j, LANES * (j + 1))
            p0[pl.ds(start + 32, 16), :] = part[0:16, lanes]
            p1[pl.ds(start + 16, 16), :] = part[16:32, lanes]
            p2[pl.ds(start, 16), :] = part[32:48, lanes]
        return carry

    steps = LEV // CHUNK
    lax.fori_loop(0, steps // 2, physics, 0)
    for d in range(4):
        pl.when(has[d] & late[d] & near[d])(functools.partial(answer, d))
    lax.fori_loop(steps // 2, steps, physics, 0)

    peers = slots.shape[1]
    column = lax.broadcasted_iota(jnp.int32, (LANES, peers), 0)
    hits = jnp.zeros((LANES, peers), jnp.float32)
    for s in range(slots.shape[0]):
        hits = jnp.where(slots[s : s + 1, :] == column, 1.0, hits)
    alive = jnp.max(hits, axis=1, keepdims=True)

    for start in range(0, FEAT, LANES):
        width = min(LANES, FEAT - start)
        rows = slice(16 + start, 16 + start + width)
        total = p0[rows, :] + p1[rows, :] + p2[rows, :]
        tend = jnp.transpose(total.astype(jnp.bfloat16), (1, 0)).astype(jnp.float32)
        tend = jnp.where(alive > 0.0, tend, 0.0)
        out[:, :, start : start + width] = own[:, :, start : start + width] + tend.reshape(ROWS, COLS, width)

    scale = -0.5 * courant
    for r in range(ROWS):
        centre = own[r]
        faces = flux(centre[:-1], centre[1:], 0)
        none = jnp.zeros((1, FEAT), jnp.float32)
        div = jnp.concatenate([faces, none], axis=0) - jnp.concatenate([none, faces], axis=0)
        out[r] = out[r] + scale * div
        if r < ROWS - 1:
            face = scale * flux(centre, own[r + 1], 1)
            out[r] = out[r] + face
            out[r + 1] = out[r + 1] - face

    def edge(d):
        if d == EAST:
            out[:, COLS - 1, :] = out[:, COLS - 1, :] + scale * flux(own[:, COLS - 1, :], halo_e[...], 0)
        elif d == WEST:
            out[:, 0, :] = out[:, 0, :] - scale * flux(halo_w[...], own[:, 0, :], 0)
        elif d == NORTH:
            out[ROWS - 1] = out[ROWS - 1] + scale * flux(own[ROWS - 1], halo_n[...], 1)
        else:
            out[0] = out[0] - scale * flux(halo_s[...], own[0], 1)

    def outside(ref):
        ref[...] = jnp.zeros_like(ref)

    pl.when(jnp.logical_not(has[NORTH]))(functools.partial(outside, halo_n))
    pl.when(jnp.logical_not(has[SOUTH]))(functools.partial(outside, halo_s))

    def arrived(d):
        sends[OPPOSITE[d]].wait_recv()

    for d in (NORTH, SOUTH, EAST, WEST):
        pl.when(has[d] & near[d])(functools.partial(arrived, d))
        pl.when(near[d])(functools.partial(edge, d))
    for d in (SOUTH, EAST, WEST):

        @pl.when(far[d])
        def _(d=d):
            answer(d)
            arrived(d)
            edge(d)

    for d in range(4):
        pl.when(has[d])(lambda d=d: sends[d].wait_send())


def shards(n_lat, n_lon, model_state, send_slots, in_weight, in_bias, mid_weight, mid_bias, out_weight):
    f32, bf16 = jnp.float32, jnp.bfloat16
    slab = (ROWS, COLS, FEAT)
    return pl.pallas_call(
        functools.partial(kernel, n_lat, n_lon),
        out_shape=pltpu.VMEM(slab, f32),
        in_specs=[pl.BlockSpec(memory_space=pl.ANY)] * 7,
        out_specs=pl.BlockSpec(memory_space=pltpu.VMEM),
        scratch_shapes=[
            pltpu.VMEM(slab, f32),
            pltpu.VMEM((send_slots.shape[3], send_slots.shape[2]), jnp.int32),
            pltpu.VMEM((3 * NVAR, HID), bf16),
            pltpu.VMEM((HID,), f32),
            pltpu.VMEM((HID, HID), bf16),
            pltpu.VMEM((HID,), f32),
            pltpu.VMEM((3, NVAR, HID), bf16),
            pltpu.VMEM((FEAT + 32, LANES), bf16),
            pltpu.VMEM((64, 512), bf16),
            pltpu.VMEM((512, 512), bf16),
            pltpu.VMEM((512, 64), bf16),
            pltpu.VMEM((512, 512), bf16),
            pltpu.VMEM((48, 512), bf16),
            pltpu.VMEM((8, 512), f32),
            pltpu.VMEM((FEAT + 32, LANES), f32),
            pltpu.VMEM((FEAT + 32, LANES), f32),
            pltpu.VMEM((FEAT + 32, LANES), f32),
            pltpu.VMEM((HPAD, CHUNK * LANES), bf16),
            pltpu.VMEM((HPAD, CHUNK * LANES), bf16),
            pltpu.VMEM((ROWS, FEAT), f32),
            pltpu.VMEM((ROWS, FEAT), f32),
            pltpu.VMEM((COLS, FEAT), f32),
            pltpu.VMEM((COLS, FEAT), f32),
            pltpu.SemaphoreType.DMA((7,)),
            pltpu.SemaphoreType.DMA((4,)),
            pltpu.SemaphoreType.DMA((4,)),
            pltpu.SemaphoreType.REGULAR((4,)),
        ],
        compiler_params=pltpu.CompilerParams(
            collective_id=0, has_side_effects=True, vmem_limit_bytes=VMEM_LIMIT
        ),
    )(
        model_state,
        jnp.transpose(send_slots.reshape(send_slots.shape[2:]), (1, 0)),
        in_weight.reshape(3 * NVAR, HID),
        in_bias,
        mid_weight,
        mid_bias,
        jnp.transpose(out_weight, (0, 2, 1)),
    )


def solution(mesh):
    return jax.shard_map(
        functools.partial(shards, mesh.shape["lat"], mesh.shape["lon"]),
        mesh=mesh,
        in_specs=(P("lat", "lon", None), P("lat", "lon", None, None), P(), P(), P(), P(), P()),
        out_specs=P("lat", "lon", None),
        check_vma=False,
    )
```

time: 29.4 us -> 22.7 us (0.77)
  the two profiles are of different devices: /device:TPU:14 before, /device:TPU:2 now
where the time goes in v2:
time: 22.7 us; the launch traced here: 22.6 us
  Pallas kernels  21.8 us (96%)
  local copies, waits for them, and re-layouts  0.8 us (4%)
    pallas_call x1, Pallas kernels, shards(): pl.pallas_call(functools.partial(kernel, n_lat, n_lon), out_shape=pltpu.V...  21.8 us
    unnamed x1, local copies, waits for them, and re-layouts  0.8 us

profile of v2, /device:TPU:2, one launch (start us, length us, event | category | flops | bytes accessed | tf_op | source)
XLA Modules:
  0.0 22.6 jit_solution(8735997830051658953)
XLA Ops:
  0.0 21.8 %shard_map.73 = f32[8,16,960]{2,1,0:T(8,128)S(1)} custom-call(f32[8,16,960]{2,1,0:T(8,128)} %state.1, s32[4,32]{1,0:T(4,128)} %bitcast.7, bf16[48,406]{1,0:T(8,128)(2,1)} %bitcast.5, f32[406]{0:T(512)} %b1_hbm.1, bf16[406,406]{1,0:T(8,128)(2,1)} %wm_hbm.1, f32[406]{0:T(512)} %bm_hbm.1, bf16[3,16,406]{2,1,0:T(8,128)(2,1)} %bitcast.6), custom_call_target="tpu_custom_call" | custom-call | tf_op jit(solution)/shard_map/pallas_call | solution.py:271
  21.8 0.8 %copy.9 = f32[8,16,960]{2,1,0:T(8,128)} copy(f32[8,16,960]{2,1,0:T(8,128)S(1)} %shard_map.73) | data formatting | bytes 983040

commit v3 on v2

--- a/solution.py
+++ b/solution.py
@@ -72,19 +72,18 @@
     def lower_first(a):
         return (lax.rem(a, 8) < 4) | (lax.rem(a, 8) == 7)
 
-    beside_root_e = (lat == 0) & last_column
     beside_root_w = (lat == 0) & (lon == 1)
     above_root = (lat == 1) & first_column
     has = (lon >= 0, lon >= 0, lat < n_lat - 1, lat > 0)
     first = (
-        root | (last_column & (lat > 0)),
-        root | ((lon > 0) & jnp.logical_not(beside_root_w)),
+        root | last_column,
+        (lon > 0) & jnp.logical_not(beside_root_w),
         root | jnp.logical_not(lower_first(lat)),
         lower_first(lat + 7) & jnp.logical_not(above_root),
     )
     far = (
-        jnp.logical_not(first[EAST]) & ((lon == half - 1) | beside_root_e),
-        jnp.logical_not(first[WEST]) & (first_column | beside_root_w),
+        jnp.logical_not(first[EAST]) & (lon == half - 1),
+        jnp.logical_not(first[WEST]) & ((first_column & jnp.logical_not(root)) | beside_root_w),
         lat < 0,
         above_root,
     )
@@ -95,9 +94,9 @@
     n_lat, n_lon,
     state, slots_hbm, w1_hbm, b1_hbm, wm_hbm, bm_hbm, wo_hbm, out,
     own, slots, w1, b1, wm, bm, wo,
-    xt, a1, am, w1t, wmt, wot, brow, p0, p1, p2, h1, h2,
+    xt, a1, am, w1t, wmt, wot, brow, p0, p1, p2, h1, h2, held, sides,
     halo_e, halo_w, halo_n, halo_s,
-    load_sem, send_sem, recv_sem, ready_sem,
+    load_sem, send_sem, recv_sem, ready_sem, side_sem,
 ):
     lat, lon = lax.axis_index("lat"), lax.axis_index("lon")
     has, first, far = neighbours(lat, lon, n_lat, n_lon)
@@ -110,6 +109,11 @@
         (lat - 1, lon),
     )
     barrier = pltpu.get_barrier_semaphore()
+    fetches = [
+        pltpu.make_async_copy(state.at[:, c, :], sides.at[n], side_sem.at[n]) for n, c in enumerate((COLS - 1, 0))
+    ]
+    for fetch in fetches:
+        fetch.start()
 
     def signal(sem, d):
         pl.semaphore_signal(sem, inc=1, device_id=where[d], device_id_type=MESH)
@@ -119,11 +123,8 @@
 
     pairs = ((state, own), (w1_hbm, w1), (b1_hbm, b1), (bm_hbm, bm), (wm_hbm, wm), (wo_hbm, wo), (slots_hbm, slots))
     loads = [pltpu.make_async_copy(src, dst, load_sem.at[n]) for n, (src, dst) in enumerate(pairs)]
-    for load in loads:
-        load.start()
-
     halos = (halo_e, halo_w, halo_n, halo_s)
-    edges = (state.at[:, COLS - 1, :], state.at[:, 0, :], state.at[ROWS - 1], state.at[0])
+    edges = (sides.at[0], sides.at[1], state.at[ROWS - 1], state.at[0])
     sends = [
         pltpu.make_async_remote_copy(
             src_ref=edges[d], dst_ref=halos[OPPOSITE[d]], send_sem=send_sem.at[d], recv_sem=recv_sem.at[OPPOSITE[d]],
@@ -134,13 +135,22 @@
     count = jnp.int32(0)
     for d in range(4):
         count = count + (has[d] & first[d]).astype(jnp.int32)
-    pl.when(count > 0)(lambda: pl.semaphore_wait(barrier, count))
-    for d in range(4):
-
-        @pl.when(has[d] & first[d])
-        def _(d=d):
-            sends[d].start()
-            signal(ready_sem.at[OPPOSITE[d]], d)
+
+    def enter():
+        for fetch in fetches:
+            fetch.wait()
+        pl.when(count > 0)(lambda: pl.semaphore_wait(barrier, count))
+        for d in (EAST, WEST, NORTH, SOUTH):
+
+            @pl.when(has[d] & first[d])
+            def _(d=d):
+                sends[d].start()
+                signal(ready_sem.at[OPPOSITE[d]], d)
+
+    across = (lat == 0) & (lon == n_lon - 1)
+    pl.when(jnp.logical_not(across))(enter)
+    for load in loads:
+        load.start()
 
     def answer(d):
         pl.semaphore_wait(ready_sem.at[d], 1)
@@ -200,6 +210,7 @@
 
     steps = LEV // CHUNK
     lax.fori_loop(0, steps // 2, physics, 0)
+    pl.when(across)(enter)
     for d in range(4):
         pl.when(has[d] & late[d] & near[d])(functools.partial(answer, d))
     lax.fori_loop(steps // 2, steps, physics, 0)
@@ -231,11 +242,14 @@
             out[r] = out[r] + face
             out[r + 1] = out[r + 1] - face
 
+    def columns(n, c):
+        held[n] = out[:, c, :]
+
     def edge(d):
         if d == EAST:
-            out[:, COLS - 1, :] = out[:, COLS - 1, :] + scale * flux(own[:, COLS - 1, :], halo_e[...], 0)
+            out[:, COLS - 1, :] = held[0] + scale * flux(sides[0], halo_e[...], 0)
         elif d == WEST:
-            out[:, 0, :] = out[:, 0, :] - scale * flux(halo_w[...], own[:, 0, :], 0)
+            out[:, 0, :] = held[1] - scale * flux(halo_w[...], sides[1], 0)
         elif d == NORTH:
             out[ROWS - 1] = out[ROWS - 1] + scale * flux(own[ROWS - 1], halo_n[...], 1)
         else:
@@ -250,14 +264,31 @@
     def arrived(d):
         sends[OPPOSITE[d]].wait_recv()
 
-    for d in (NORTH, SOUTH, EAST, WEST):
+    for d in (NORTH, SOUTH):
         pl.when(has[d] & near[d])(functools.partial(arrived, d))
         pl.when(near[d])(functools.partial(edge, d))
-    for d in (SOUTH, EAST, WEST):
+
+    @pl.when(far[SOUTH])
+    def _():
+        answer(SOUTH)
+        arrived(SOUTH)
+        edge(SOUTH)
+
+    columns(0, COLS - 1)
+    columns(1, 0)
+    for d in (EAST, WEST):
+
+        @pl.when(near[d])
+        def _(d=d):
+            arrived(d)
+            edge(d)
+
+    for d in (EAST, WEST):
 
         @pl.when(far[d])
         def _(d=d):
-            answer(d)
+            pl.semaphore_wait(ready_sem.at[d], 1)
+            sends[d].start()
             arrived(d)
             edge(d)
 
@@ -293,6 +324,8 @@
             pltpu.VMEM((FEAT + 32, LANES), f32),
             pltpu.VMEM((HPAD, CHUNK * LANES), bf16),
             pltpu.VMEM((HPAD, CHUNK * LANES), bf16),
+            pltpu.VMEM((2, ROWS, FEAT), f32),
+            pltpu.VMEM((2, ROWS, FEAT), f32),
             pltpu.VMEM((ROWS, FEAT), f32),
             pltpu.VMEM((ROWS, FEAT), f32),
             pltpu.VMEM((COLS, FEAT), f32),
@@ -301,6 +334,7 @@
             pltpu.SemaphoreType.DMA((4,)),
             pltpu.SemaphoreType.DMA((4,)),
             pltpu.SemaphoreType.REGULAR((4,)),
+            pltpu.SemaphoreType.DMA((2,)),
         ],
         compiler_params=pltpu.CompilerParams(
             collective_id=0, has_side_effects=True, vmem_limit_bytes=VMEM_LIMIT

time: 22.7 us -> 20.2 us (0.89)
  the two profiles are of different devices: /device:TPU:2 before, /device:TPU:14 now
where the time goes in v3:
time: 20.2 us; the launch traced here: 20 us
  Pallas kernels  19.2 us (95%)
  local copies, waits for them, and re-layouts  0.8 us (4%)
    pallas_call x1, Pallas kernels, shards(): pl.pallas_call(functools.partial(kernel, n_lat, n_lon), out_shape=pltpu.V...  19.2 us
    unnamed x1, local copies, waits for them, and re-layouts  0.8 us

profile of v3, /device:TPU:14, one launch (start us, length us, event | category | flops | bytes accessed | tf_op | source)
XLA Modules:
  0.0 20.0 jit_solution(13877053213511736222)
XLA Ops:
  0.0 19.2 %shard_map.73 = f32[8,16,960]{2,1,0:T(8,128)S(1)} custom-call(f32[8,16,960]{2,1,0:T(8,128)} %state.1, s32[4,32]{1,0:T(4,128)} %bitcast.7, bf16[48,406]{1,0:T(8,128)(2,1)} %bitcast.5, f32[406]{0:T(512)} %b1_hbm.1, bf16[406,406]{1,0:T(8,128)(2,1)} %wm_hbm.1, f32[406]{0:T(512)} %bm_hbm.1, bf16[3,16,406]{2,1,0:T(8,128)(2,1)} %bitcast.6), custom_call_target="tpu_custom_call" | custom-call | tf_op jit(solution)/shard_map/pallas_call | solution.py:302
  19.2 0.8 %copy.9 = f32[8,16,960]{2,1,0:T(8,128)} copy(f32[8,16,960]{2,1,0:T(8,128)S(1)} %shard_map.73) | data formatting | bytes 983040

commit v4 on v3

--- a/solution.py
+++ b/solution.py
@@ -76,8 +76,8 @@
     above_root = (lat == 1) & first_column
     has = (lon >= 0, lon >= 0, lat < n_lat - 1, lat > 0)
     first = (
-        root | last_column,
-        (lon > 0) & jnp.logical_not(beside_root_w),
+        root | last_column | (lon == n_lon - 2),
+        (lon > 0) & jnp.logical_not(last_column | beside_root_w),
         root | jnp.logical_not(lower_first(lat)),
         lower_first(lat + 7) & jnp.logical_not(above_root),
     )
@@ -109,47 +109,47 @@
         (lat - 1, lon),
     )
     barrier = pltpu.get_barrier_semaphore()
+    last_column = lon == n_lon - 1
+    direct = (lon >= 0, lon >= 0, jnp.logical_not(last_column), jnp.logical_not(last_column))
     fetches = [
         pltpu.make_async_copy(state.at[:, c, :], sides.at[n], side_sem.at[n]) for n, c in enumerate((COLS - 1, 0))
     ]
-    for fetch in fetches:
-        fetch.start()
 
     def signal(sem, d):
         pl.semaphore_signal(sem, inc=1, device_id=where[d], device_id_type=MESH)
 
     for d in range(4):
-        pl.when(has[d] & late[d])(functools.partial(signal, barrier, d))
+        pl.when(has[d] & late[d] & direct[d])(functools.partial(signal, barrier, d))
 
     pairs = ((state, own), (w1_hbm, w1), (b1_hbm, b1), (bm_hbm, bm), (wm_hbm, wm), (wo_hbm, wo), (slots_hbm, slots))
     loads = [pltpu.make_async_copy(src, dst, load_sem.at[n]) for n, (src, dst) in enumerate(pairs)]
     halos = (halo_e, halo_w, halo_n, halo_s)
-    edges = (sides.at[0], sides.at[1], state.at[ROWS - 1], state.at[0])
-    sends = [
-        pltpu.make_async_remote_copy(
-            src_ref=edges[d], dst_ref=halos[OPPOSITE[d]], send_sem=send_sem.at[d], recv_sem=recv_sem.at[OPPOSITE[d]],
+    edges = (state.at[:, COLS - 1, :], state.at[:, 0, :], state.at[ROWS - 1], state.at[0])
+
+    def send(d, src):
+        return pltpu.make_async_remote_copy(
+            src_ref=src, dst_ref=halos[OPPOSITE[d]], send_sem=send_sem.at[d], recv_sem=recv_sem.at[OPPOSITE[d]],
             device_id=where[d], device_id_type=MESH,
         )
-        for d in range(4)
-    ]
+
+    sends = [send(d, edges[d]) for d in range(4)]
+    replies = [send(EAST, sides.at[0]), send(WEST, sides.at[1])]
     count = jnp.int32(0)
     for d in range(4):
-        count = count + (has[d] & first[d]).astype(jnp.int32)
+        count = count + (has[d] & first[d] & direct[d]).astype(jnp.int32)
 
     def enter():
-        for fetch in fetches:
-            fetch.wait()
         pl.when(count > 0)(lambda: pl.semaphore_wait(barrier, count))
         for d in (EAST, WEST, NORTH, SOUTH):
 
-            @pl.when(has[d] & first[d])
+            @pl.when(has[d] & first[d] & direct[d])
             def _(d=d):
                 sends[d].start()
                 signal(ready_sem.at[OPPOSITE[d]], d)
 
     across = (lat == 0) & (lon == n_lon - 1)
     pl.when(jnp.logical_not(across))(enter)
-    for load in loads:
+    for load in loads + fetches:
         load.start()
 
     def answer(d):
@@ -160,7 +160,7 @@
     am[...] = jnp.zeros_like(am)
     wot[...] = jnp.zeros_like(wot)
     brow[...] = jnp.zeros_like(brow)
-    for load in loads[1:]:
+    for load in loads[1:] + fetches:
         load.wait()
     brow[0:1, 0:HID] = b1[...].reshape(1, HID) * 0.5
     brow[1:2, 0:HID] = bm[...].reshape(1, HID) * 0.5
@@ -212,7 +212,22 @@
     lax.fori_loop(0, steps // 2, physics, 0)
     pl.when(across)(enter)
     for d in range(4):
-        pl.when(has[d] & late[d] & near[d])(functools.partial(answer, d))
+
+        @pl.when(has[d] & late[d] & near[d] & direct[d])
+        def _(d=d):
+            answer(d)
+            if d in (NORTH, SOUTH):
+                pl.when(lon == n_lon - 2)(functools.partial(signal, ready_sem.at[d], EAST))
+
+    for d in (NORTH, SOUTH):
+
+        @pl.when(has[d] & late[d] & last_column)
+        def _(d=d):
+            answer(d)
+            signal(ready_sem.at[OPPOSITE[d]], d)
+
+    for d in (NORTH, SOUTH):
+        pl.when(has[d] & first[d] & last_column)(functools.partial(answer, d))
     lax.fori_loop(steps // 2, steps, physics, 0)
 
     peers = slots.shape[1]
@@ -288,7 +303,7 @@
         @pl.when(far[d])
         def _(d=d):
             pl.semaphore_wait(ready_sem.at[d], 1)
-            sends[d].start()
+            replies[d].start()
             arrived(d)
             edge(d)
 

time: 20.2 us -> 19.6 us (0.970)
  Pallas kernels: 19.2 us -> 18.7 us
    pallas_call x1, Pallas kernels: 19.2 us -> 18.7 us  [shards(): pl.pallas_call(functools.partial(kernel, n_lat, n_lon), out_shape=pltpu.V...]
where the time goes in v4:
time: 19.6 us; the launch traced here: 19.5 us
  Pallas kernels  18.7 us (95%)
  local copies, waits for them, and re-layouts  0.8 us (4%)
    pallas_call x1, Pallas kernels, shards(): pl.pallas_call(functools.partial(kernel, n_lat, n_lon), out_shape=pltpu.V...  18.7 us
    unnamed x1, local copies, waits for them, and re-layouts  0.8 us

profile of v4, /device:TPU:14, one launch (start us, length us, event | category | flops | bytes accessed | tf_op | source)
XLA Modules:
  0.0 19.5 jit_solution(16812608578022992987)
XLA Ops:
  0.0 18.7 %shard_map.73 = f32[8,16,960]{2,1,0:T(8,128)S(1)} custom-call(f32[8,16,960]{2,1,0:T(8,128)} %state.1, s32[4,32]{1,0:T(4,128)} %bitcast.7, bf16[48,406]{1,0:T(8,128)(2,1)} %bitcast.5, f32[406]{0:T(512)} %b1_hbm.1, bf16[406,406]{1,0:T(8,128)(2,1)} %wm_hbm.1, f32[406]{0:T(512)} %bm_hbm.1, bf16[3,16,406]{2,1,0:T(8,128)(2,1)} %bitcast.6), custom_call_target="tpu_custom_call" | custom-call | tf_op jit(solution)/shard_map/pallas_call | solution.py:317
  18.7 0.8 %copy.9 = f32[8,16,960]{2,1,0:T(8,128)} copy(f32[8,16,960]{2,1,0:T(8,128)S(1)} %shard_map.73) | data formatting | bytes 983040

commit v5 on v4

--- a/solution.py
+++ b/solution.py
@@ -118,11 +118,7 @@
     def signal(sem, d):
         pl.semaphore_signal(sem, inc=1, device_id=where[d], device_id_type=MESH)
 
-    for d in range(4):
-        pl.when(has[d] & late[d] & direct[d])(functools.partial(signal, barrier, d))
-
-    pairs = ((state, own), (w1_hbm, w1), (b1_hbm, b1), (bm_hbm, bm), (wm_hbm, wm), (wo_hbm, wo), (slots_hbm, slots))
-    loads = [pltpu.make_async_copy(src, dst, load_sem.at[n]) for n, (src, dst) in enumerate(pairs)]
+
     halos = (halo_e, halo_w, halo_n, halo_s)
     edges = (state.at[:, COLS - 1, :], state.at[:, 0, :], state.at[ROWS - 1], state.at[0])
 
@@ -148,7 +144,17 @@
                 signal(ready_sem.at[OPPOSITE[d]], d)
 
     across = (lat == 0) & (lon == n_lon - 1)
-    pl.when(jnp.logical_not(across))(enter)
+    @pl.when(last_column & jnp.logical_not(across))
+    def _():
+        pl.semaphore_wait(barrier, 1)
+        sends[EAST].start()
+        signal(ready_sem.at[WEST], EAST)
+
+    for d in range(4):
+        pl.when(has[d] & late[d] & direct[d])(functools.partial(signal, barrier, d))
+    pl.when(jnp.logical_not(last_column))(enter)
+    pairs = ((state, own), (w1_hbm, w1), (b1_hbm, b1), (bm_hbm, bm), (wm_hbm, wm), (wo_hbm, wo), (slots_hbm, slots))
+    loads = [pltpu.make_async_copy(src, dst, load_sem.at[n]) for n, (src, dst) in enumerate(pairs)]
     for load in loads + fetches:
         load.start()
 
@@ -298,6 +304,10 @@
             arrived(d)
             edge(d)
 
+    for d in range(4):
+        pl.when(has[d] & near[d])(lambda d=d: sends[d].wait_send())
+    pl.when(far[SOUTH])(lambda: sends[SOUTH].wait_send())
+
     for d in (EAST, WEST):
 
         @pl.when(far[d])
@@ -306,9 +316,7 @@
             replies[d].start()
             arrived(d)
             edge(d)
-
-    for d in range(4):
-        pl.when(has[d])(lambda d=d: sends[d].wait_send())
+            replies[d].wait_send()
 
 
 def shards(n_lat, n_lon, model_state, send_slots, in_weight, in_bias, mid_weight, mid_bias, out_weight):

time: 19.6 us -> 19.6 us (level)
  no operation moved by 1% of the time
where the time goes in v5:
time: 19.6 us; the launch traced here: 19.4 us
  Pallas kernels  18.6 us (95%)
  local copies, waits for them, and re-layouts  0.8 us (4%)
    pallas_call x1, Pallas kernels, shards(): pl.pallas_call(functools.partial(kernel, n_lat, n_lon), out_shape=pltpu.V...  18.6 us
    unnamed x1, local copies, waits for them, and re-layouts  0.8 us

profile of v5, /device:TPU:14, one launch (start us, length us, event | category | flops | bytes accessed | tf_op | source)
XLA Modules:
  0.0 19.4 jit_solution(16249364396121361313)
XLA Ops:
  0.0 18.6 %shard_map.73 = f32[8,16,960]{2,1,0:T(8,128)S(1)} custom-call(f32[8,16,960]{2,1,0:T(8,128)} %state.1, s32[4,32]{1,0:T(4,128)} %bitcast.7, bf16[48,406]{1,0:T(8,128)(2,1)} %bitcast.5, f32[406]{0:T(512)} %b1_hbm.1, bf16[406,406]{1,0:T(8,128)(2,1)} %wm_hbm.1, f32[406]{0:T(512)} %bm_hbm.1, bf16[3,16,406]{2,1,0:T(8,128)(2,1)} %bitcast.6), custom_call_target="tpu_custom_call" | custom-call | tf_op jit(solution)/shard_map/pallas_call | solution.py:325
  18.7 0.8 %copy.9 = f32[8,16,960]{2,1,0:T(8,128)} copy(f32[8,16,960]{2,1,0:T(8,128)S(1)} %shard_map.73) | data formatting | bytes 983040

commit v6 on v5

--- a/solution.py
+++ b/solution.py
@@ -99,25 +99,20 @@
     load_sem, send_sem, recv_sem, ready_sem, side_sem,
 ):
     lat, lon = lax.axis_index("lat"), lax.axis_index("lon")
-    has, first, far = neighbours(lat, lon, n_lat, n_lon)
-    late = [jnp.logical_not(f) for f in first]
-    near = [jnp.logical_not(f) for f in far]
     where = (
         (lat, lax.rem(lon + 1, n_lon)),
         (lat, lax.rem(lon + n_lon - 1, n_lon)),
-        (lat + 1, lon),
-        (lat - 1, lon),
+        (jnp.minimum(lat + 1, n_lat - 1), lon),
+        (jnp.maximum(lat - 1, 0), lon),
     )
     barrier = pltpu.get_barrier_semaphore()
     last_column = lon == n_lon - 1
-    direct = (lon >= 0, lon >= 0, jnp.logical_not(last_column), jnp.logical_not(last_column))
     fetches = [
         pltpu.make_async_copy(state.at[:, c, :], sides.at[n], side_sem.at[n]) for n, c in enumerate((COLS - 1, 0))
     ]
 
     def signal(sem, d):
         pl.semaphore_signal(sem, inc=1, device_id=where[d], device_id_type=MESH)
-
 
     halos = (halo_e, halo_w, halo_n, halo_s)
     edges = (state.at[:, COLS - 1, :], state.at[:, 0, :], state.at[ROWS - 1], state.at[0])
@@ -130,25 +125,30 @@
 
     sends = [send(d, edges[d]) for d in range(4)]
     replies = [send(EAST, sides.at[0]), send(WEST, sides.at[1])]
-    count = jnp.int32(0)
-    for d in range(4):
-        count = count + (has[d] & first[d] & direct[d]).astype(jnp.int32)
-
-    def enter():
-        pl.when(count > 0)(lambda: pl.semaphore_wait(barrier, count))
-        for d in (EAST, WEST, NORTH, SOUTH):
-
-            @pl.when(has[d] & first[d] & direct[d])
-            def _(d=d):
-                sends[d].start()
-                signal(ready_sem.at[OPPOSITE[d]], d)
-
-    across = (lat == 0) & (lon == n_lon - 1)
+    across = (lat == 0) & last_column
+
     @pl.when(last_column & jnp.logical_not(across))
     def _():
         pl.semaphore_wait(barrier, 1)
         sends[EAST].start()
         signal(ready_sem.at[WEST], EAST)
+
+    has, first, far = neighbours(lat, lon, n_lat, n_lon)
+    late = [jnp.logical_not(f) for f in first]
+    near = [jnp.logical_not(f) for f in far]
+    direct = (lon >= 0, lon >= 0, jnp.logical_not(last_column), jnp.logical_not(last_column))
+    count = jnp.int32(0)
+    for d in range(4):
+        count = count + (has[d] & first[d] & direct[d]).astype(jnp.int32)
+
+    def enter():
+        pl.when(count > 0)(lambda: pl.semaphore_wait(barrier, count))
+        for d in (EAST, WEST, NORTH, SOUTH):
+
+            @pl.when(has[d] & first[d] & direct[d])
+            def _(d=d):
+                sends[d].start()
+                signal(ready_sem.at[OPPOSITE[d]], d)
 
     for d in range(4):
         pl.when(has[d] & late[d] & direct[d])(functools.partial(signal, barrier, d))

time: 19.6 us -> 19.6 us (level)
  no operation moved by 1% of the time
where the time goes in v6:
time: 19.6 us; the launch traced here: 19.4 us
  Pallas kernels  18.6 us (95%)
  local copies, waits for them, and re-layouts  0.8 us (4%)
    pallas_call x1, Pallas kernels, shards(): pl.pallas_call(functools.partial(kernel, n_lat, n_lon), out_shape=pltpu.V...  18.6 us
    unnamed x1, local copies, waits for them, and re-layouts  0.8 us

profile of v6, /device:TPU:14, one launch (start us, length us, event | category | flops | bytes accessed | tf_op | source)
XLA Modules:
  0.0 19.4 jit_solution(10693559072698789756)
XLA Ops:
  0.0 18.6 %shard_map.73 = f32[8,16,960]{2,1,0:T(8,128)S(1)} custom-call(f32[8,16,960]{2,1,0:T(8,128)} %state.1, s32[4,32]{1,0:T(4,128)} %bitcast.7, bf16[48,406]{1,0:T(8,128)(2,1)} %bitcast.5, f32[406]{0:T(512)} %b1_hbm.1, bf16[406,406]{1,0:T(8,128)(2,1)} %wm_hbm.1, f32[406]{0:T(512)} %bm_hbm.1, bf16[3,16,406]{2,1,0:T(8,128)(2,1)} %bitcast.6), custom_call_target="tpu_custom_call" | custom-call | tf_op jit(solution)/shard_map/pallas_call | solution.py:325
  18.6 0.8 %copy.9 = f32[8,16,960]{2,1,0:T(8,128)} copy(f32[8,16,960]{2,1,0:T(8,128)S(1)} %shard_map.73) | data formatting | bytes 983040

commit v7 on v6

--- a/solution.py
+++ b/solution.py
@@ -155,8 +155,6 @@
     pl.when(jnp.logical_not(last_column))(enter)
     pairs = ((state, own), (w1_hbm, w1), (b1_hbm, b1), (bm_hbm, bm), (wm_hbm, wm), (wo_hbm, wo), (slots_hbm, slots))
     loads = [pltpu.make_async_copy(src, dst, load_sem.at[n]) for n, (src, dst) in enumerate(pairs)]
-    for load in loads + fetches:
-        load.start()
 
     def answer(d):
         pl.semaphore_wait(ready_sem.at[d], 1)
@@ -166,6 +164,11 @@
     am[...] = jnp.zeros_like(am)
     wot[...] = jnp.zeros_like(wot)
     brow[...] = jnp.zeros_like(brow)
+    p0[...] = jnp.zeros_like(p0)
+    p1[...] = jnp.zeros_like(p1)
+    p2[...] = jnp.zeros_like(p2)
+    for load in loads + fetches:
+        load.start()
     for load in loads[1:] + fetches:
         load.wait()
     brow[0:1, 0:HID] = b1[...].reshape(1, HID) * 0.5
@@ -187,9 +190,6 @@
         width = min(LANES, FEAT - start)
         xt[16 + start : 16 + start + width, :] = jnp.transpose(cells[:, start : start + width], (1, 0))
 
-    p0[...] = jnp.zeros_like(p0)
-    p1[...] = jnp.zeros_like(p1)
-    p2[...] = jnp.zeros_like(p2)
     ones = jnp.ones((16, LANES), jnp.bfloat16)
     last_row = lax.broadcasted_iota(jnp.int32, (16, CHUNK * LANES), 0)
     is_one = (last_row >= 6) & (last_row < 9)

time: 19.6 us -> 19.6 us (level)
  no operation moved by 1% of the time
where the time goes in v7:
time: 19.6 us; the launch traced here: 19.4 us
  Pallas kernels  18.6 us (95%)
  local copies, waits for them, and re-layouts  0.8 us (4%)
    pallas_call x1, Pallas kernels, shards(): pl.pallas_call(functools.partial(kernel, n_lat, n_lon), out_shape=pltpu.V...  18.6 us
    unnamed x1, local copies, waits for them, and re-layouts  0.8 us

profile of v7, /device:TPU:14, one launch (start us, length us, event | category | flops | bytes accessed | tf_op | source)
XLA Modules:
  0.0 19.4 jit_solution(3333510434138246013)
XLA Ops:
  0.0 18.6 %shard_map.73 = f32[8,16,960]{2,1,0:T(8,128)S(1)} custom-call(f32[8,16,960]{2,1,0:T(8,128)} %state.1, s32[4,32]{1,0:T(4,128)} %bitcast.7, bf16[48,406]{1,0:T(8,128)(2,1)} %bitcast.5, f32[406]{0:T(512)} %b1_hbm.1, bf16[406,406]{1,0:T(8,128)(2,1)} %wm_hbm.1, f32[406]{0:T(512)} %bm_hbm.1, bf16[3,16,406]{2,1,0:T(8,128)(2,1)} %bitcast.6), custom_call_target="tpu_custom_call" | custom-call | tf_op jit(solution)/shard_map/pallas_call | solution.py:325
  18.6 0.8 %copy.9 = f32[8,16,960]{2,1,0:T(8,128)} copy(f32[8,16,960]{2,1,0:T(8,128)S(1)} %shard_map.73) | data formatting | bytes 983040
